TPU v7x, 32 devices: a whole 2x2x4 slice. The times are simulated.
32 devices in a mesh: gx: 4 (over x, core), gy: 8 (over z, y).
Axes of the slice: x: 2, y: 2, z: 4, core: 2. Of those that a mesh axis runs over, the one named last changes fastest.
Arguments:
- activation: bfloat16 [32, 16, 32, 128], P(None, 'gx', 'gy'), may hold values from -6 to 6
- out_grad: bfloat16 [32, 16, 32, 128], P(None, 'gx', 'gy'), may hold values from -6 to 6
- kernel: bfloat16 [3, 3, 3, 32, 32], replicated, may hold values from -0.21875 to 0.21875
Outputs:
- grad_input: bfloat16 [32, 16, 32, 128], P(None, 'gx', 'gy')
- grad_kernel: float32 [3, 3, 3, 32, 32], replicated
All inputs are finite; a program needn't handle non-finite values.
Results may differ from a plain program's by a relative error of at most 0.001.
Values may be sent and summed in bfloat16 or wider, within the bound.
No kernel may reach another device: no remote copies, remote signals or barrier semaphores. Data moves between devices by JAX's collectives and lax.ppermute only.
A program may use at most 64 MiB of HBM per device.

v0:
```python
import jax
import jax.numpy as jnp
from jax import lax
from jax.sharding import PartitionSpec as P


def extended(cells, sides, width):
    for axis, dim in sides:
        count = lax.axis_size(axis)
        ends = count - 1
        head = lax.slice_in_dim(cells, 0, width, axis=dim)
        tail = lax.slice_in_dim(cells, cells.shape[dim] - width, cells.shape[dim], axis=dim)
        cells = jnp.concatenate(
            [
                lax.ppermute(tail, axis, [(i, (i + 1) % count) for i in range(ends)]),
                cells,
                lax.ppermute(head, axis, [((i + 1) % count, i) for i in range(ends)]),
            ],
            axis=dim,
        )
    return cells


def padded_z(block):
    return jnp.pad(block, ((0, 0), (0, 0), (0, 0), (1, 1)))


def contract_cells(left, right):
    return lax.dot_general(
        left, right, (((1,), (1,)), ((), ())), preferred_element_type=jnp.float32
    )


def shards(activation, out_grad, kernel):
    channels = activation.shape[0]
    size_x, size_y, size_z = (activation.shape[1], activation.shape[2], activation.shape[3])
    cell_count = size_x * size_y * size_z
    grad_pad = padded_z(extended(out_grad, (("gx", 1), ("gy", 2)), 1))
    flat_act = activation.reshape(channels, cell_count)
    accumulated = jnp.zeros((channels, cell_count), jnp.float32)
    products = []
    for off_x in range(3):
        for off_y in range(3):
            for off_z in range(3):
                window = grad_pad[
                    :,
                    2 - off_x : 2 - off_x + size_x,
                    2 - off_y : 2 - off_y + size_y,
                    2 - off_z : 2 - off_z + size_z,
                ].reshape(channels, cell_count)
                accumulated = accumulated + jnp.dot(
                    kernel[off_x, off_y, off_z].T, window, preferred_element_type=jnp.float32
                )
                products.append(contract_cells(window, flat_act))
    grad_input = accumulated.reshape(channels, size_x, size_y, size_z).astype(jnp.bfloat16)
    local_terms = jnp.stack(products).reshape(3, 3, 3, channels, channels)
    summed = lax.psum(local_terms, ("gx", "gy"))
    total_cells = size_x * lax.axis_size("gx") * size_y * lax.axis_size("gy") * size_z
    grad_kernel = summed / jnp.sqrt(jnp.float32(total_cells))
    return (grad_input, grad_kernel)


def solution(mesh):
    return jax.shard_map(
        shards,
        mesh=mesh,
        in_specs=(P(None, "gx", "gy", None), P(None, "gx", "gy", None), P()),
        out_specs=(P(None, "gx", "gy", None), P()),
        check_vma=False,
    )
```

profile of v0, /device:TPU:8, one launch (start us, length us, event | category | flops | bytes accessed | tf_op | source)
XLA Modules:
  0.0 171.7 jit_solution(9164996284599008277)
XLA Ops:
  8.1 1.7 %collective-permute-start = (bf16[32,1,4,128]{3,0,2,1:T(8,128)(2,1)S(1)}, bf16[32,1,4,128]{3,0,2,1:T(8,128)(2,1)S(1)}, u32[]{:S(2)}, u32[]{:S(2)}) collective-permute-start(bf16[32,1,4,128]{3,0,2,1:T(8,128)(2,1)S(1)} %copy.183), channel_id=1, source_target_pairs={{0,8},{8,16},{16,24},{1,9},{9,17},{17,25},{2,10},{10,18},{18,26},{... | collective-permute-start | bytes 98312 | tf_op jit(solution)/shard_map/ppermute | solution.py:15
  9.9 1.3 collective-permute-start.1
  11.2 1.6 reshape.104
  12.9 1.3 collective-permute-done.1
  14.3 3.4 %collective-permute-start.2 = (bf16[32,6,1,128]{3,0,2,1:T(8,128)(2,1)S(1)}, bf16[32,6,1,128]{3,0,2,1:T(8,128)(2,1)S(1)}, u32[]{:S(2)}, u32[]{:S(2)}) collective-permute-start(bf16[32,6,1,128]{3,0,2,1:T(8,128)(2,1)S(1)} %get-tuple-element.29), channel_id=1, source_target_pairs={{0,1},{1,2},{2,3},{3,4},{4,5},{5,6},{6,7},{8,9},{9,10},{10,11},{11... | collective-permute-start | bytes 147464 | tf_op jit(solution)/shard_map/ppermute | solution.py:15
  17.7 3.3 %collective-permute-start.3 = (bf16[32,6,1,128]{3,0,2,1:T(8,128)(2,1)S(1)}, bf16[32,6,1,128]{3,0,2,1:T(8,128)(2,1)S(1)}, u32[]{:S(2)}, u32[]{:S(2)}) collective-permute-start(bf16[32,6,1,128]{3,0,2,1:T(8,128)(2,1)S(1)} %get-tuple-element.30), channel_id=1, source_target_pairs={{1,0},{2,1},{3,2},{4,3},{5,4},{6,5},{7,6},{9,8},{10,9},{11,10},{12... | collective-permute-start | bytes 147464 | tf_op jit(solution)/shard_map/ppermute | solution.py:17
  24.0 1.3 fusion.161
  53.3 1.1 convolution_bitcast_fusion.10
  55.2 1.0 reshape.110
  57.1 1.2 convolution_add_fusion.12
  58.3 1.0 convolution_add_fusion.11
  59.3 1.0 convolution_add_fusion.10
  60.3 1.0 convolution_add_fusion.9
  61.3 1.0 convolution_add_fusion.8
  62.3 1.0 convolution_add_fusion.7
  63.3 1.0 convolution_add_fusion.6
  64.3 1.0 convolution_add_fusion.5
  65.2 1.0 convolution_add_fusion.4
  66.2 1.0 convolution_add_fusion.3
  67.2 1.0 convolution_add_fusion.2
  68.2 1.0 fusion.13
  70.1 1.0 fusion.14
  71.9 91.1 %all-reduce.3.cloned.1.call-done = f32[3,3,3,32,32]{4,3,2,1,0:T(8,128)} async-done(((f32[3,3,3,32,32]{4,3,2,1,0:T(8,128)}), f32[3,3,3,32,32]{4,3,2,1,0:T(8,128)}) %all-reduce.3.cloned.1.call-update) | async-done | bytes 110608 | tf_op jit(solution)/shard_map/psum | solution.py:57
  163.0 1.8 %broadcast_multiply_fusion = f32[3,3,3,32,32]{4,3,2,1,0:T(8,128)} fusion(f32[3,3,3,32,32]{4,3,2,1,0:T(8,128)} %all-reduce.3.cloned.1.call-done), kind=kLoop, calls=%fused_computation.117 | loop fusion | flops 27648 | bytes 221184 | tf_op jit(solution)/shard_map/div | solution.py:59
  (150 shorter events, 35.1 us)
Async XLA Ops:
  7.2 18.1 %copy-start = (bf16[32,4,4,128]{3,2,1,0:T(4,128)(2,1)S(1)}, bf16[32,4,4,128]{3,2,1,0:T(4,128)(2,1)}, u32[]{:S(2)}) copy-start(bf16[32,4,4,128]{3,2,1,0:T(4,128)(2,1)} %param.3) | copy-start | bytes 393220
  7.2 5.6 %copy-start.1 = (bf16[32,4,4,128]{3,2,1,0:T(4,128)(2,1)S(1)}, bf16[32,4,4,128]{3,2,1,0:T(4,128)(2,1)}, u32[]{:S(2)}) copy-start(bf16[32,4,4,128]{3,2,1,0:T(4,128)(2,1)} %param.4) | copy-start | bytes 393220
  7.2 155.8 %all-reduce.3.cloned.1.call-start = ((), (), s32[]{:S(2)}) async-start(), calls=%async_computation | async-start | bytes 884736 | tf_op jit(solution)/shard_map/psum | solution.py:57
  8.1 4.7 %collective-permute-start = (bf16[32,1,4,128]{3,0,2,1:T(8,128)(2,1)S(1)}, bf16[32,1,4,128]{3,0,2,1:T(8,128)(2,1)S(1)}, u32[]{:S(2)}, u32[]{:S(2)}) collective-permute-start(bf16[32,1,4,128]{3,0,2,1:T(8,128)(2,1)S(1)} %copy.183), channel_id=1, source_target_pairs={{0,8},{8,16},{16,24},{1,9},{9,17},{17,25},{2,10},{10,18},{18,26},{... | collective-permute-start | bytes 98312 | tf_op jit(solution)/shard_map/ppermute | solution.py:15
  9.9 4.4 %collective-permute-start.1 = (bf16[32,1,4,128]{3,0,2,1:T(8,128)(2,1)S(1)}, bf16[32,1,4,128]{3,0,2,1:T(8,128)(2,1)S(1)}, u32[]{:S(2)}, u32[]{:S(2)}) collective-permute-start(bf16[32,1,4,128]{3,0,2,1:T(8,128)(2,1)S(1)} %copy.184), channel_id=1, source_target_pairs={{8,0},{16,8},{24,16},{9,1},{17,9},{25,17},{10,2},{18,10},{26,18},{... | collective-permute-start | bytes 98312 | tf_op jit(solution)/shard_map/ppermute | solution.py:17
  14.3 8.7 %collective-permute-start.2 = (bf16[32,6,1,128]{3,0,2,1:T(8,128)(2,1)S(1)}, bf16[32,6,1,128]{3,0,2,1:T(8,128)(2,1)S(1)}, u32[]{:S(2)}, u32[]{:S(2)}) collective-permute-start(bf16[32,6,1,128]{3,0,2,1:T(8,128)(2,1)S(1)} %get-tuple-element.29), channel_id=1, source_target_pairs={{0,1},{1,2},{2,3},{3,4},{4,5},{5,6},{6,7},{8,9},{9,10},{10,11},{11... | collective-permute-start | bytes 147464 | tf_op jit(solution)/shard_map/ppermute | solution.py:15
  17.7 6.0 %collective-permute-start.3 = (bf16[32,6,1,128]{3,0,2,1:T(8,128)(2,1)S(1)}, bf16[32,6,1,128]{3,0,2,1:T(8,128)(2,1)S(1)}, u32[]{:S(2)}, u32[]{:S(2)}) collective-permute-start(bf16[32,6,1,128]{3,0,2,1:T(8,128)(2,1)S(1)} %get-tuple-element.30), channel_id=1, source_target_pairs={{1,0},{2,1},{3,2},{4,3},{5,4},{6,5},{7,6},{9,8},{10,9},{11,10},{12... | collective-permute-start | bytes 147464 | tf_op jit(solution)/shard_map/ppermute | solution.py:17
  33.2 1.6 copy-start.3
  35.6 1.6 copy-start.7
  49.6 1.8 %copy-start.4 = (bf16[32,4,4,128]{3,0,2,1:T(8,128)(2,1)S(1)}, bf16[32,4,4,128]{3,0,2,1:T(8,128)(2,1)}, u32[]{:S(2)}) copy-start(bf16[32,4,4,128]{3,0,2,1:T(8,128)(2,1)} %get-tuple-element.26) | copy-start | bytes 393220
  50.7 1.8 %copy-start.2 = (bf16[32,4,4,128]{3,0,2,1:T(8,128)(2,1)S(1)}, bf16[32,4,4,128]{3,0,2,1:T(8,128)(2,1)}, u32[]{:S(2)}) copy-start(bf16[32,4,4,128]{3,0,2,1:T(8,128)(2,1)} %get-tuple-element.27) | copy-start | bytes 393220
  56.2 2.2 %copy-start.11 = (bf16[32,2048]{1,0:T(8,128)(2,1)S(1)}, bf16[32,2048]{1,0:T(8,128)(2,1)}, u32[]{:S(2)}) copy-start(bf16[32,2048]{1,0:T(8,128)(2,1)} %reshape.93) | copy-start | bytes 393220
  57.1 2.2 %copy-start.13 = (bf16[32,2048]{1,0:T(8,128)(2,1)S(1)}, bf16[32,2048]{1,0:T(8,128)(2,1)}, u32[]{:S(2)}) copy-start(bf16[32,2048]{1,0:T(8,128)(2,1)} %reshape.94) | copy-start | bytes 393220
  58.3 2.0 %copy-start.9 = (bf16[32,2048]{1,0:T(8,128)(2,1)S(1)}, bf16[32,2048]{1,0:T(8,128)(2,1)}, u32[]{:S(2)}) copy-start(bf16[32,2048]{1,0:T(8,128)(2,1)} %reshape.95) | copy-start | bytes 393220
  59.3 2.0 %copy-start.10 = (bf16[32,2048]{1,0:T(8,128)(2,1)S(1)}, bf16[32,2048]{1,0:T(8,128)(2,1)}, u32[]{:S(2)}) copy-start(bf16[32,2048]{1,0:T(8,128)(2,1)} %reshape.96) | copy-start | bytes 393220
  60.3 2.0 %copy-start.12 = (bf16[32,2048]{1,0:T(8,128)(2,1)S(1)}, bf16[32,2048]{1,0:T(8,128)(2,1)}, u32[]{:S(2)}) copy-start(bf16[32,2048]{1,0:T(8,128)(2,1)} %reshape.97) | copy-start | bytes 393220
  61.3 2.0 %copy-start.14 = (bf16[32,2048]{1,0:T(8,128)(2,1)S(1)}, bf16[32,2048]{1,0:T(8,128)(2,1)}, u32[]{:S(2)}) copy-start(bf16[32,2048]{1,0:T(8,128)(2,1)} %reshape.98) | copy-start | bytes 393220
  62.3 2.0 %copy-start.15 = (bf16[32,2048]{1,0:T(8,128)(2,1)S(1)}, bf16[32,2048]{1,0:T(8,128)(2,1)}, u32[]{:S(2)}) copy-start(bf16[32,2048]{1,0:T(8,128)(2,1)} %reshape.99) | copy-start | bytes 393220
  63.3 2.0 %copy-start.16 = (bf16[32,2048]{1,0:T(8,128)(2,1)S(1)}, bf16[32,2048]{1,0:T(8,128)(2,1)}, u32[]{:S(2)}) copy-start(bf16[32,2048]{1,0:T(8,128)(2,1)} %reshape.100) | copy-start | bytes 393220
  64.2 2.0 %copy-start.17 = (bf16[32,2048]{1,0:T(8,128)(2,1)S(1)}, bf16[32,2048]{1,0:T(8,128)(2,1)}, u32[]{:S(2)}) copy-start(bf16[32,2048]{1,0:T(8,128)(2,1)} %reshape.101) | copy-start | bytes 393220
  65.2 2.0 %copy-start.18 = (bf16[32,2048]{1,0:T(8,128)(2,1)S(1)}, bf16[32,2048]{1,0:T(8,128)(2,1)}, u32[]{:S(2)}) copy-start(bf16[32,2048]{1,0:T(8,128)(2,1)} %reshape.102) | copy-start | bytes 393220
  66.2 2.0 %copy-start.19 = (bf16[32,2048]{1,0:T(8,128)(2,1)S(1)}, bf16[32,2048]{1,0:T(8,128)(2,1)}, u32[]{:S(2)}) copy-start(bf16[32,2048]{1,0:T(8,128)(2,1)} %reshape.103) | copy-start | bytes 393220
  67.2 2.0 %copy-start.8 = (bf16[32,2048]{1,0:T(8,128)(2,1)S(1)}, bf16[32,2048]{1,0:T(8,128)(2,1)}, u32[]{:S(2)}) copy-start(bf16[32,2048]{1,0:T(8,128)(2,1)} %reshape.104) | copy-start | bytes 393220
  68.2 1.9 %copy-start.6 = (bf16[32,2048]{1,0:T(8,128)(2,1)S(1)}, bf16[32,2048]{1,0:T(8,128)(2,1)}, u32[]{:S(2)}) copy-start(bf16[32,2048]{1,0:T(8,128)(2,1)} %reshape.105) | copy-start | bytes 393220
  (2 other events, 2.4 us)
Sparse Core Ops, SparseCore 0:
  31.4 131.5 all-reduce.2
where the time goes:
time: 173 us; the launch traced here: 172 us
  waiting for transfers between devices  93.2 us (54%)
  matrix products  31 us (18%)
  local copies, waits for them, and re-layouts  19.9 us (12%)
  between operations  14.8 us (9%)
  starting transfers between devices  9.81 us (6%)
  other arithmetic  2.88 us (2%)
    psum x1, waiting for transfers between devices, shards(): summed = lax.psum(local_terms, ('gx', 'gy'))  91.1 us
    dot_general x27, matrix products, shards(): jnp.dot(kernel[off_x, off_y, off_z].T, window, preferred_element_type=jnp...  25.8 us
    reshape x27, local copies, waits for them, and re-layouts, shards(): window = grad_pad[:, 2 - off_x:2 - off_x + size_x, 2 - off_y:2 - off_y +...  13.6 us
    dot_general x27, matrix products, contract_cells(): lax.dot_general(left, right, (((1,), (1,)), ((), ())), preferred_element_...  5.22 us
    ppermute x2, starting transfers between devices, extended(): lax.ppermute(tail, axis, [(i, (i + 1) % count) for i in range(ends)])  5.17 us
    ppermute x2, starting transfers between devices, extended(): lax.ppermute(head, axis, [((i + 1) % count, i) for i in range(ends)])  4.61 us
    slice x29, local copies, waits for them, and re-layouts, shards(): grad_pad[:, 2 - off_x:2 - off_x + size_x, 2 - off_y:2 - off_y + size_y, 2...  3.73 us
  transfers between devices with their start and end apart: 5, of which 3 were waited for; matrix products, arithmetic and copies ran while one was open for 25% of the time, Pallas kernels for 0%

commit v1 on v0

--- a/solution.py
+++ b/solution.py
@@ -54,7 +54,8 @@
                 products.append(contract_cells(window, flat_act))
     grad_input = accumulated.reshape(channels, size_x, size_y, size_z).astype(jnp.bfloat16)
     local_terms = jnp.stack(products).reshape(3, 3, 3, channels, channels)
-    summed = lax.psum(local_terms, ("gx", "gy"))
+    shards_2 = lax.all_gather(local_terms, ("gx", "gy"))
+    summed = jnp.sum(shards_2, axis=0)
     total_cells = size_x * lax.axis_size("gx") * size_y * lax.axis_size("gy") * size_z
     grad_kernel = summed / jnp.sqrt(jnp.float32(total_cells))
     return (grad_input, grad_kernel)

time: 173 us -> 151 us (0.87)
  matrix products: 31 us -> 14.2 us
  waiting for transfers between devices: 93.2 us -> 76.7 us
  other arithmetic: 2.88 us -> 9.62 us
  local copies, waits for them, and re-layouts: 19.9 us -> 24.6 us
    psum x1 -> x0, waiting for transfers between devices: 91.1 us -> none  [shards(): summed = lax.psum(local_terms, ('gx', 'gy'))]
    all_gather x0 -> x1, waiting for transfers between devices: none -> 72.1 us  [shards(): shards_2 = lax.all_gather(local_terms, ('gx', 'gy'))]
    dot_general x27, matrix products: 25.8 us -> 8.94 us  [shards(): jnp.dot(kernel[off_x, off_y, off_z].T, window, preferred_element_type=jnp...]
    reduce_sum x0 -> x1, other arithmetic: none -> 6.85 us  [shards(): summed = jnp.sum(shards_2, axis=0)]
    slice x29, local copies, waits for them, and re-layouts: 3.73 us -> 9.21 us  [shards(): grad_pad[:, 2 - off_x:2 - off_x + size_x, 2 - off_y:2 - off_y + size_y, 2...]
    ppermute x2, waiting for transfers between devices: 0.01 us -> 2.62 us  [extended(): lax.ppermute(tail, axis, [(i, (i + 1) % count) for i in range(ends)])]
  transfers between devices with their start and end apart: 5 -> 5, of which waited for: 3 -> 3; matrix products, arithmetic and copies ran while one was open for 25% -> 23% of each run, Pallas kernels for 0% -> 0%
where the time goes in v1:
time: 151 us; the launch traced here: 149 us
  waiting for transfers between devices  76.7 us (51%)
  local copies, waits for them, and re-layouts  24.6 us (16%)
  between operations  14.7 us (10%)
  matrix products  14.2 us (9%)
  other arithmetic  9.62 us (6%)
  starting transfers between devices  8.91 us (6%)
    all_gather x1, waiting for transfers between devices, shards(): shards_2 = lax.all_gather(local_terms, ('gx', 'gy'))  72.1 us
    reshape x27, local copies, waits for them, and re-layouts, shards(): window = grad_pad[:, 2 - off_x:2 - off_x + size_x, 2 - off_y:2 - off_y +...  11.9 us
    slice x29, local copies, waits for them, and re-layouts, shards(): grad_pad[:, 2 - off_x:2 - off_x + size_x, 2 - off_y:2 - off_y + size_y, 2...  9.21 us
    dot_general x27, matrix products, shards(): jnp.dot(kernel[off_x, off_y, off_z].T, window, preferred_element_type=jnp...  8.94 us
    reduce_sum x1, other arithmetic, shards(): summed = jnp.sum(shards_2, axis=0)  6.85 us
    dot_general x27, matrix products, contract_cells(): lax.dot_general(left, right, (((1,), (1,)), ((), ())), preferred_element_...  5.23 us
    ppermute x2, starting transfers between devices, extended(): lax.ppermute(head, axis, [((i + 1) % count, i) for i in range(ends)])  4.61 us
    ppermute x2, starting transfers between devices, extended(): lax.ppermute(tail, axis, [(i, (i + 1) % count) for i in range(ends)])  4.27 us
  transfers between devices with their start and end apart: 5, of which 3 were waited for; matrix products, arithmetic and copies ran while one was open for 23% of the time, Pallas kernels for 0%

profile of v1, /device:TPU:8, one launch (start us, length us, event | category | flops | bytes accessed | tf_op | source)
XLA Modules:
  0.0 148.7 jit_solution(11209371832599699137)
XLA Ops:
  8.1 1.7 %collective-permute-start = (bf16[32,1,4,128]{3,0,2,1:T(8,128)(2,1)S(1)}, bf16[32,1,4,128]{3,0,2,1:T(8,128)(2,1)S(1)}, u32[]{:S(2)}, u32[]{:S(2)}) collective-permute-start(bf16[32,1,4,128]{3,0,2,1:T(8,128)(2,1)S(1)} %copy.242), channel_id=1, source_target_pairs={{0,8},{8,16},{16,24},{1,9},{9,17},{17,25},{2,10},{10,18},{18,26},{... | collective-permute-start | bytes 98312 | tf_op jit(solution)/shard_map/ppermute | solution.py:15
  9.9 1.3 collective-permute-start.1
  11.2 1.0 constant_dynamic-update-slice_fusion.4
  12.2 2.0 %collective-permute-done.1 = bf16[32,1,4,128]{3,0,2,1:T(8,128)(2,1)S(1)} collective-permute-done((bf16[32,1,4,128]{3,0,2,1:T(8,128)(2,1)S(1)}, bf16[32,1,4,128]{3,0,2,1:T(8,128)(2,1)S(1)}, u32[]{:S(2)}, u32[]{:S(2)}) %collective-permute-start.1) | collective-permute-done | bytes 32800 | tf_op jit(solution)/shard_map/ppermute | solution.py:17
  14.3 3.3 %collective-permute-start.3 = (bf16[32,6,1,128]{3,0,2,1:T(8,128)(2,1)S(1)}, bf16[32,6,1,128]{3,0,2,1:T(8,128)(2,1)S(1)}, u32[]{:S(2)}, u32[]{:S(2)}) collective-permute-start(bf16[32,6,1,128]{3,0,2,1:T(8,128)(2,1)S(1)} %get-tuple-element.30), channel_id=1, source_target_pairs={{1,0},{2,1},{3,2},{4,3},{5,4},{6,5},{7,6},{9,8},{10,9},{11,10},{12... | collective-permute-start | bytes 147464 | tf_op jit(solution)/shard_map/ppermute | solution.py:17
  17.6 2.5 %collective-permute-start.2 = (bf16[32,6,1,128]{3,0,2,1:T(8,128)(2,1)S(1)}, bf16[32,6,1,128]{3,0,2,1:T(8,128)(2,1)S(1)}, u32[]{:S(2)}, u32[]{:S(2)}) collective-permute-start(bf16[32,6,1,128]{3,0,2,1:T(8,128)(2,1)S(1)} %get-tuple-element.29), channel_id=1, source_target_pairs={{0,1},{1,2},{2,3},{3,4},{4,5},{5,6},{6,7},{8,9},{9,10},{10,11},{11... | collective-permute-start | bytes 147464 | tf_op jit(solution)/shard_map/ppermute | solution.py:15
  21.9 2.6 %collective-permute-done.2 = bf16[32,6,1,128]{3,0,2,1:T(8,128)(2,1)S(1)} collective-permute-done((bf16[32,6,1,128]{3,0,2,1:T(8,128)(2,1)S(1)}, bf16[32,6,1,128]{3,0,2,1:T(8,128)(2,1)S(1)}, u32[]{:S(2)}, u32[]{:S(2)}) %collective-permute-start.2) | collective-permute-done | bytes 49184 | tf_op jit(solution)/shard_map/ppermute | solution.py:15
  30.8 0.9 convolution_bitcast_fusion.4
  31.8 1.2 fusion.161
  33.2 1.7 %fusion.52 = (bf16[32,4,4,128]{3,0,2,1:T(8,128)(2,1)S(1)}, bf16[32,4,4,128]{3,0,2,1:T(8,128)(2,1)S(1)}, bf16[32,4,4,128]{3,0,2,1:T(8,128)(2,1)}, bf16[32,4,4,128...) fusion(bf16[32,6,4,128]{3,0,2,1:T(8,128)(2,1)S(1)} %get-tuple-element.37, ...), kind=kLoop, calls=%fused_computation.122 | loop fusion | flops 393216 | bytes 1081344 | tf_op jit(solution)/shard_map/concatenate | solution.py:13
  36.2 1.0 reshape.108
  37.2 1.6 %copy.119 = bf16[32,4,4,128]{3,2,1,0:T(4,128)(2,1)} copy(bf16[32,4,4,128]{3,0,2,1:T(8,128)(2,1)} %get-tuple-element.22) | data formatting | bytes 262144 | tf_op jit(solution)/shard_map/slice | solution.py:45
  38.9 1.0 reshape.107
  40.6 1.0 reshape.106
  42.3 1.0 reshape.105
  44.0 1.0 reshape.104
  45.7 1.0 reshape.103
  47.4 1.0 reshape.88
  49.1 1.6 %reshape.89 = bf16[32,2048]{1,0:T(8,128)(2,1)} reshape(bf16[32,4,4,128]{3,2,1,0:T(4,128)(2,1)} %copy.101) | data formatting | bytes 262144 | tf_op jit(solution)/shard_map/reshape | solution.py:50
  53.1 1.0 convolution_bitcast_fusion
  54.1 0.9 convolution_bitcast_fusion.1
  55.1 0.9 convolution_bitcast_fusion.2
  62.2 72.1 %all-gather.2.cloned.1.call-done = f32[32,3,3,3,32,32]{5,4,3,2,1,0:T(8,128)} async-done(((f32[1,3,3,3,32,32]{5,4,3,2,1,0:T(8,128)}), f32[32,3,3,3,32,32]{5,4,3,2,1,0:T(8,128)}) %all-gather.2.cloned.1.call-update) | async-done | bytes 3538960 | tf_op jit(solution)/shard_map/all_gather | solution.py:57
  134.2 6.9 %reduce_sum.9 = f32[3,3,3,32,32]{4,3,2,1,0:T(8,128)S(1)} reduce(f32[32,3,3,3,32,32]{5,4,3,2,1,0:T(8,128)} %all-gather.2.cloned.1.call-done, f32[]{:T(128)} %constant.6.clone.1), dimensions={0}, to_apply=%region_0.1 | reduce | flops 857088 | bytes 3649540 | tf_op jit(solution)/shard_map/reduce_sum | solution.py:58
  (135 shorter events, 23.8 us)
Async XLA Ops:
  7.2 17.6 %copy-start = (bf16[32,4,4,128]{3,2,1,0:T(4,128)(2,1)S(1)}, bf16[32,4,4,128]{3,2,1,0:T(4,128)(2,1)}, u32[]{:S(2)}) copy-start(bf16[32,4,4,128]{3,2,1,0:T(4,128)(2,1)} %param.3) | copy-start | bytes 393220
  7.2 13.0 %copy-start.1 = (bf16[32,4,4,128]{3,2,1,0:T(4,128)(2,1)S(1)}, bf16[32,4,4,128]{3,2,1,0:T(4,128)(2,1)}, u32[]{:S(2)}) copy-start(bf16[32,4,4,128]{3,2,1,0:T(4,128)(2,1)} %param.4) | copy-start | bytes 393220
  7.2 127.1 %all-gather.2.cloned.1.call-start = ((), (), s32[]{:S(2)}) async-start(), calls=%async_computation | async-start | bytes 14598144 | tf_op jit(solution)/shard_map/all_gather | solution.py:57
  8.1 3.1 %collective-permute-start = (bf16[32,1,4,128]{3,0,2,1:T(8,128)(2,1)S(1)}, bf16[32,1,4,128]{3,0,2,1:T(8,128)(2,1)S(1)}, u32[]{:S(2)}, u32[]{:S(2)}) collective-permute-start(bf16[32,1,4,128]{3,0,2,1:T(8,128)(2,1)S(1)} %copy.242), channel_id=1, source_target_pairs={{0,8},{8,16},{16,24},{1,9},{9,17},{17,25},{2,10},{10,18},{18,26},{... | collective-permute-start | bytes 98312 | tf_op jit(solution)/shard_map/ppermute | solution.py:15
  9.9 4.4 %collective-permute-start.1 = (bf16[32,1,4,128]{3,0,2,1:T(8,128)(2,1)S(1)}, bf16[32,1,4,128]{3,0,2,1:T(8,128)(2,1)S(1)}, u32[]{:S(2)}, u32[]{:S(2)}) collective-permute-start(bf16[32,1,4,128]{3,0,2,1:T(8,128)(2,1)S(1)} %copy.243), channel_id=1, source_target_pairs={{8,0},{16,8},{24,16},{9,1},{17,9},{25,17},{10,2},{18,10},{26,18},{... | collective-permute-start | bytes 98312 | tf_op jit(solution)/shard_map/ppermute | solution.py:17
  14.3 7.6 %collective-permute-start.3 = (bf16[32,6,1,128]{3,0,2,1:T(8,128)(2,1)S(1)}, bf16[32,6,1,128]{3,0,2,1:T(8,128)(2,1)S(1)}, u32[]{:S(2)}, u32[]{:S(2)}) collective-permute-start(bf16[32,6,1,128]{3,0,2,1:T(8,128)(2,1)S(1)} %get-tuple-element.30), channel_id=1, source_target_pairs={{1,0},{2,1},{3,2},{4,3},{5,4},{6,5},{7,6},{9,8},{10,9},{11,10},{12... | collective-permute-start | bytes 147464 | tf_op jit(solution)/shard_map/ppermute | solution.py:17
  17.6 6.9 %collective-permute-start.2 = (bf16[32,6,1,128]{3,0,2,1:T(8,128)(2,1)S(1)}, bf16[32,6,1,128]{3,0,2,1:T(8,128)(2,1)S(1)}, u32[]{:S(2)}, u32[]{:S(2)}) collective-permute-start(bf16[32,6,1,128]{3,0,2,1:T(8,128)(2,1)S(1)} %get-tuple-element.29), channel_id=1, source_target_pairs={{0,1},{1,2},{2,3},{3,4},{4,5},{5,6},{6,7},{8,9},{9,10},{10,11},{11... | collective-permute-start | bytes 147464 | tf_op jit(solution)/shard_map/ppermute | solution.py:15
  21.9 6.7 %copy-start.11 = (bf16[32,6,1,128]{3,0,2,1:T(8,128)(2,1)}, bf16[32,6,1,128]{3,0,2,1:T(8,128)(2,1)S(1)}, u32[]{:S(2)}) copy-start(bf16[32,6,1,128]{3,0,2,1:T(8,128)(2,1)S(1)} %collective-permute-done.3) | copy-start | bytes 147460
  24.5 5.2 %copy-start.12 = (bf16[32,6,1,128]{3,0,2,1:T(8,128)(2,1)}, bf16[32,6,1,128]{3,0,2,1:T(8,128)(2,1)S(1)}, u32[]{:S(2)}) copy-start(bf16[32,6,1,128]{3,0,2,1:T(8,128)(2,1)S(1)} %collective-permute-done.2) | copy-start | bytes 147460
  30.0 0.8 copy-start.9
  33.0 2.0 %copy-start.4 = (bf16[32,4,4,128]{3,0,2,1:T(8,128)(2,1)S(1)}, bf16[32,4,4,128]{3,0,2,1:T(8,128)(2,1)}, u32[]{:S(2)}) copy-start(bf16[32,4,4,128]{3,0,2,1:T(8,128)(2,1)} %get-tuple-element.3) | copy-start | bytes 393220
  33.1 2.1 %copy-start.2 = (bf16[32,4,4,128]{3,0,2,1:T(8,128)(2,1)S(1)}, bf16[32,4,4,128]{3,0,2,1:T(8,128)(2,1)}, u32[]{:S(2)}) copy-start(bf16[32,4,4,128]{3,0,2,1:T(8,128)(2,1)} %get-tuple-element.4) | copy-start | bytes 393220
  35.4 7.8 %copy-start.3 = (bf16[32,4,4,128]{3,0,2,1:T(8,128)(2,1)S(1)}, bf16[32,4,4,128]{3,0,2,1:T(8,128)(2,1)}, u32[]{:S(2)}) copy-start(bf16[32,4,4,128]{3,0,2,1:T(8,128)(2,1)} %get-tuple-element.27) | copy-start | bytes 393220
  53.1 2.9 %copy-start.10 = (bf16[3,3,3,32,32]{4,3,2,1,0:T(8,128)(2,1)S(1)}, bf16[3,3,3,32,32]{4,3,2,1,0:T(8,128)(2,1)}, u32[]{:S(2)}) copy-start(bf16[3,3,3,32,32]{4,3,2,1,0:T(8,128)(2,1)} %param.5) | copy-start | bytes 165892
  56.7 1.4 copy-start.7
  57.1 1.2 copy-start.8
  57.8 0.9 copy-start.6
  59.9 0.9 copy-start.5
Sparse Core Ops, SparseCore 0:
  30.9 103.2 all-gather.1
